TPU v7x, 256 devices: a whole 4x4x8 slice. The times are simulated.
256 devices in a mesh: seg: 4 (over y_hi, core), mic: 64 (over z, x, y_lo).
Axes of the slice: x: 4, y: 4 (y_hi: 2, y_lo: 2; y = y_hi * 2 + y_lo), z: 8, core: 2. Of those that a mesh axis runs over, the one named last changes fastest.
Arguments:
- time_data: bfloat16 [128, 4096, 1024], P('seg', 'mic'), may hold values from -6 to 6
- order_bin: int32 [1], replicated, may hold values from 32 to 203
- mic_pos: int32 [3, 4096], replicated, may hold values from -2000 to 2000
- grid_pos: int32 [3, 131072], P(None, 'mic'), may hold values from -1500 to 1500
Outputs:
- beam_power: float32 [64, 2048], P('mic', 'seg')
All inputs are finite; a program needn't handle non-finite values.
Results may differ from a plain program's by a relative error of at most 0.00083.
Values may be sent and summed in bfloat16 or wider, within the bound.
A program may use at most 256 MiB of HBM per device.

v0:
```python
import math

import jax
import jax.numpy as jnp
from jax import lax
from jax.sharding import PartitionSpec as P


def spectral_table(order_value, samples):
    times = jnp.arange(samples, dtype=jnp.int32)
    turned = order_value * times % samples
    angle = turned.astype(jnp.float32) * (2.0 * math.pi / samples)
    window = 0.5 - 0.5 * jnp.cos(times.astype(jnp.float32) * (2.0 * math.pi / samples))
    return jnp.stack([window * jnp.cos(angle), -(window * jnp.sin(angle))]).astype(jnp.bfloat16)


def stacked_left(spectra):
    real_part = spectra[0]
    imag_part = spectra[1]
    upper = jnp.concatenate([real_part, -imag_part], axis=1)
    lower = jnp.concatenate([imag_part, real_part], axis=1)
    return jnp.concatenate([upper, lower], axis=0)


def beam_block(left, mic_part, points, wave):
    offsets = (points[:, None, :] - mic_part[:, :, None]).astype(jnp.float32) * 0.001
    distance = jnp.sqrt(offsets[0] * offsets[0] + offsets[1] * offsets[1] + offsets[2] * offsets[2])
    phase = wave * distance
    steering = jnp.concatenate([jnp.cos(phase), jnp.sin(phase)], axis=0).astype(jnp.bfloat16)
    return jnp.dot(left, steering, preferred_element_type=jnp.float32)


def make_folder(points, mic_pos, wave):

    def accumulate(carry, piece, start):
        left = stacked_left(piece)
        return beam_block(left, mic_pos, points, wave)

    return accumulate


def shards(time_data, order_bin, mic_pos, grid_pos):
    seg_dev = time_data.shape[0]
    mic_dev = time_data.shape[1]
    samples = time_data.shape[2]
    table = spectral_table(order_bin[0], samples)
    rows = time_data.reshape(seg_dev * mic_dev, samples)
    spec = jnp.dot(rows, table.T, preferred_element_type=jnp.float32)
    spectra = spec.T.reshape(2, seg_dev, mic_dev).astype(jnp.bfloat16)
    wave = (
        order_bin[0].astype(jnp.float32)
        * jnp.float32(2.0 * math.pi * 51200.0 / 343.0)
        / jnp.float32(samples)
    )
    seg_count = lax.axis_size("seg")
    seg_total = seg_count * seg_dev
    mic_total = lax.axis_size("mic") * mic_dev
    denom = jnp.float32(seg_total * mic_total * 0.375 * samples)
    slab_width = grid_pos.shape[1]
    own_width = slab_width // seg_count
    folder = make_folder(grid_pos, mic_pos, wave)
    empty = jnp.zeros((2 * seg_dev, slab_width), jnp.float32)
    beams = folder(empty, lax.all_gather(spectra, "mic", axis=2, tiled=True), jnp.int32(0))
    partial_power = jnp.sum(beams * beams, axis=0) / denom
    beam_power = lax.psum_scatter(partial_power, "seg", scatter_dimension=0, tiled=True)
    return beam_power.reshape(1, own_width)


def solution(mesh):
    placed = (P("seg", "mic", None), P(), P(), P(None, "mic"))
    return jax.shard_map(
        shards, mesh=mesh, in_specs=placed, out_specs=P("mic", "seg"), check_vma=False
    )
```

profile of v0, /device:TPU:1, one launch (start us, length us, event | category | flops | bytes accessed | tf_op | source)
XLA Modules:
  0.0 471.5 jit_solution(192973803990093008)
XLA Ops:
  0.0 32.1 %convert_multiply_fusion = f32[3,4096,2048]{2,1,0:T(8,128)} fusion(s32[3,4096]{1,0:T(4,128)} %param.6, s32[3,2048]{1,0:T(4,128)} %param.7), kind=kLoop, calls=%fused_computation | loop fusion | flops 75497472 | bytes 100737024 | tf_op jit(solution)/shard_map/mul | solution.py:26
  32.8 124.3 %fusion.8 = (bf16[4096,2048]{1,0:T(8,128)(2,1)}, f32[1,4096,2048]{2,1,0:T(8,128)S(1)}) fusion(f32[3,4096,2048]{2,1,0:T(8,128)} %convert_multiply_fusion, f32[]{:T(128)S(6)} %div.9), kind=kLoop, calls=%fused_computation.14 | loop fusion | flops 58720256 | bytes 150994944 | tf_op jit(solution)/shard_map/convert
  157.1 0.0 copy-start
  157.1 108.2 %fusion.9 = bf16[4096,2048]{1,0:T(8,128)(2,1)} fusion(f32[1,4096,2048]{2,1,0:T(8,128)S(1)} %get-tuple-element.6), kind=kLoop, calls=%fused_computation.15 | loop fusion | flops 8388608 | bytes 50331648 | tf_op jit(solution)/shard_map/convert.1
  265.3 0.3 negate_convert_fusion
  265.5 0.0 copy-done
  265.5 1.7 convolution_convert_fusion
  267.3 0.1 copy.6
  267.4 144.7 %all_gather.3 = bf16[2,32,4096]{1,0,2:T(2,128)(2,1)S(1)} all-gather(bf16[2,32,64]{1,0,2:T(2,128)(2,1)S(1)} %copy.6), channel_id=1, replica_groups=mesh['seg'=4,'mic'=64] {'mic'}, dimensions={2}, use_global_device_ids=true | all-gather | bytes 532480 | tf_op jit(solution)/shard_map/all_gather | solution.py:63
  412.1 3.8 fusion.31
  415.9 0.0 copy-start.1
  415.9 4.5 copy.9
  420.4 2.1 copy.10
  422.5 12.7 %fusion.13 = f32[2048]{0:T(1024)S(1)} fusion(bf16[4096,2048]{1,0:T(8,128)(2,1)} %fusion.9, bf16[4096,2048]{1,0:T(8,128)(2,1)} %get-tuple-element.5, bf16[32,4096]{1,0:T(8,128)(2,1)S(1)} %bitcast.17, bf16[32,4096]{1,0:T(8,128)(2,1)S(1)} %bitcast.16, bf16[32,4096]{1,0:T(8,128)(2,1)S(1)} %bitcast_negate_fusion), kind=kOutput, calls=%fused_computation.17 | convolution fusion | flops 2219046912 | bytes 34349056 | tf_op jit(solution)/shard_map/dot_general | solution.py:30
  435.3 34.3 %all-reduce = f32[2048]{0:T(1024)S(1)} all-reduce(f32[2048]{0:T(1024)S(1)} %broadcast_multiply_fusion), channel_id=2, replica_groups=mesh['seg'=4,'mic'=64] {'seg'}, use_global_device_ids=true, to_apply=%region_1.2.clone | all-reduce | flops 2048 | bytes 16384
  469.6 0.0 copy-done.1
  469.6 0.6 dynamic-slice
  470.9 0.7 dynamic-slice.1
  (2 shorter events, 0.0 us)
Async XLA Ops:
  157.1 108.5 %copy-start = (bf16[32,64,1024]{2,1,0:T(8,128)(2,1)S(1)}, bf16[32,64,1024]{2,1,0:T(8,128)(2,1)}, u32[]{:S(2)}) copy-start(bf16[32,64,1024]{2,1,0:T(8,128)(2,1)} %param.4) | copy-start | bytes 12582916
  415.9 53.7 %copy-start.1 = (u32[256]{0:T(256)S(1)}, u32[256]{0:T(256)}, u32[]{:S(2)}) copy-start(u32[256]{0:T(256)} %constant.33) | copy-start | bytes 3076
where the time goes:
time: 472 us
  other arithmetic  265 us (56%)
  blocking collectives  179 us (38%)
  matrix products  14.5 us (3%)
  local copies, waits for them, and re-layouts  11.7 us (2%)
    another operation x3, other arithmetic  233 us
    all_gather x1, blocking collectives, shards(): lax.all_gather(spectra, 'mic', axis=2, tiled=True)  145 us
    unnamed x1, blocking collectives  34.3 us
    mul x1, other arithmetic, beam_block(): (points[:, None, :] - mic_part[:, :, None]).astype(jnp.float32) * 0.001  32.1 us
    dot_general x1, matrix products, beam_block(): return jnp.dot(left, steering, preferred_element_type=jnp.float32)  12.7 us

commit v1 on v0

v1 whole, which is shorter than its diff:
```python
import functools
import math

import jax
import jax.numpy as jnp
from jax import lax
from jax.experimental import pallas as pl
from jax.experimental.pallas import tpu as pltpu
from jax.sharding import PartitionSpec as P

MESH = pl.DeviceIdType.MESH
F32 = jnp.float32
BF16 = jnp.bfloat16

NX, NY, NZ = 4, 4, 8
SIN = (4.442882834149665, -7.308241154529405, 3.6062889579421076, -0.8457635944249917, 0.10920575020378133)
COS = (1.414213496564824, -6.978850988209009, 5.739461169968767, -1.8835629820109427, 0.3106981797730274)
SIN_SHORT = (4.442867902991959, -7.3074434197428175, 3.5947880638880885, -0.7843739922969518)
COS_SHORT = (1.4142040804388327, -6.977642054046934, 5.715238359077324, -1.728348549561637)


def horner(coefs, z):
    total = jnp.full_like(z, coefs[-1])
    for c in coefs[-2::-1]:
        total = total * z + c
    return total


def cos_sin_turns(turns, sin_coefs, cos_coefs):
    r = turns - jnp.round(turns)
    z = r * r
    s = r * horner(sin_coefs, z)
    c = horner(cos_coefs, z)
    return 1.0 - s * s, s * c


def device(y, z, x, core):
    return {"seg": (y // 2) * 2 + core, "mic": (z * NX + x) * 2 + y % 2}


def kernel(
    time_ref, bin_ref, mic_ref, grid_ref, out_ref,
    tbuf, wt, own, inbox, gathered, cosb, sinb, accp, accq, micf, pointf,
    t_sem, p_send, p_recv, z_send, z_recv, m_send, m_recv, l_send, l_recv, f_send, f_recv,
):
    seg = lax.axis_index("seg")
    mic = lax.axis_index("mic")
    core = seg % 2
    y_hi, y_lo = seg // 2, mic % 2
    y = y_hi * 2 + y_lo
    x = (mic // 2) % NX
    z = mic // (2 * NX)
    sibling = device(y, z, x, 1 - core)
    z_peer = [device(y, (z + d) % NZ, x, core) for d in range(NZ)]
    x_peer = [device(y, z, (x + d) % NX, core) for d in range(NX)]
    y_peer = [device((y + d) % NY, z, x, core) for d in range(NY)]

    barrier = pltpu.get_barrier_semaphore()
    peers = [sibling] + z_peer[1:] + x_peer[1:] + y_peer[1:]
    for peer in peers:
        pl.semaphore_signal(barrier, inc=1, device_id=peer, device_id_type=MESH)

    seg_dev, mic_dev, samples = time_ref.shape
    chunks = tbuf.shape[0]
    per = seg_dev // chunks

    def time_copy(i):
        return pltpu.make_async_copy(time_ref.at[pl.ds(i * per, per)], tbuf.at[i], t_sem.at[i])

    for i in range(chunks):
        time_copy(i).start()

    order = bin_ref[0]
    t = lax.broadcasted_iota(jnp.int32, (8, samples), 1)
    turned = (order * t) & (samples - 1)
    inv = 1.0 / samples
    wcos, _ = cos_sin_turns(t.astype(F32) * inv, SIN, COS)
    ca, sa = cos_sin_turns(turned.astype(F32) * inv, SIN, COS)
    window = 0.5 - 0.5 * wcos
    row_re = (window * ca).astype(BF16).astype(F32)
    row_im = (-(window * sa)).astype(BF16).astype(F32)
    wt[...] = jnp.concatenate([row_re] * 8 + [row_im] * 8, axis=0).astype(BF16)

    def split(v):
        coarse = jnp.floor(v * (1.0 / 64.0) + 0.5) * 64.0
        return coarse, v - coarse

    def split3(v):
        top = jnp.floor(v * (1.0 / 65536.0)) * 65536.0
        rest = v - top
        mid = jnp.floor(rest * (1.0 / 256.0)) * 256.0
        return top, mid, rest - mid

    width = out_ref.shape[1]
    pts = grid_ref[:, pl.ds(pl.multiple_of(seg * width, 128), width)].astype(F32)
    mics = mic_ref[...].astype(F32)

    def rows_of(v, fold):
        hi, lo = split(v)
        sq = v * v
        top, mid, low = split3(sq[0:1] + sq[1:2] + sq[2:3])
        one = jnp.ones_like(top)
        tiny = jnp.full_like(top, 2.0**-20)
        zero = jnp.zeros((13, v.shape[1]), F32)
        if fold:
            return jnp.concatenate([-2.0 * hi, -2.0 * hi, -2.0 * lo, -2.0 * lo, one, one, one, top, mid, low, tiny, zero], axis=0)
        return jnp.concatenate([hi, lo, hi, lo, top, mid, low, one, one, one, tiny, zero], axis=0)

    micf[...] = rows_of(mics, True).astype(BF16)
    pointf[...] = rows_of(pts, False).T.astype(BF16)
    turns_per_mm = order.astype(F32) * F32(0.001 * 51200.0 / 343.0 / samples)

    lane = lax.broadcasted_iota(jnp.int32, (mic_dev, 128), 1) & 63

    def spectrum(i, acc):
        time_copy(i).wait()
        part = lax.dot_general(
            tbuf[i].reshape(per * mic_dev, samples), wt[...], (((1,), (1,)), ((), ())),
            preferred_element_type=F32,
        )
        for k in range(per):
            hit = lane == core * seg_dev + i * per + k
            acc = jnp.where(hit, part[k * mic_dev:(k + 1) * mic_dev], acc)
        return acc

    acc = lax.fori_loop(0, chunks, spectrum, jnp.zeros((mic_dev, 128), F32))
    own[...] = acc.astype(BF16).reshape(4, 16, 128)

    half = pl.ds(2 * core, 2)
    pl.semaphore_wait(barrier, len(peers))

    def push(src, dst, send, recv, peer):
        return pltpu.make_async_remote_copy(
            src_ref=src, dst_ref=dst, send_sem=send, recv_sem=recv, device_id=peer, device_id_type=MESH
        )

    pair = push(own.at[pl.ds(2 * (1 - core), 2)], inbox, p_send, p_recv, sibling)
    pair.start()

    blocks = cosb.shape[2] // 256
    tall = 128

    def steer(j, carry):
        g = j // blocks
        at = pl.ds(pl.multiple_of((j % blocks) * 256, 256), 256)
        feat = micf[:, pl.ds(pl.multiple_of(j * 256, 256), 256)]
        for i in range(width // tall):
            rows = pl.ds(i * tall, tall)
            d2 = jnp.dot(pointf[rows, :], feat, preferred_element_type=F32)
            turns = (d2 * turns_per_mm) * lax.rsqrt(d2)
            ca, sa = cos_sin_turns(turns, SIN_SHORT, COS_SHORT)
            cosb[g, rows, at] = ca.astype(BF16)
            sinb[g, rows, at] = sa.astype(BF16)
        return carry

    lax.fori_loop(0, 2, steer, 0)
    pair.wait()
    mine = gathered.at[y_hi, z, x, y_lo, half]
    mine[...] = own[half] + inbox[...]

    z_out = []
    for d in range(1, NZ):
        c = push(mine, mine, z_send.at[d], z_recv.at[d], z_peer[d])
        c.start()
        z_out.append(c)
    lax.fori_loop(2, 5, steer, 0)
    for d in range(1, NZ):
        src = gathered.at[y_hi, (z + NZ - d) % NZ, x, y_lo, half]
        push(src, src, z_send.at[d], z_recv.at[d], z_peer[d]).wait_recv()

    q1, q2 = 2 * core, 2 * core + 1
    m_out = []
    for d in range(1, NX):
        line = gathered.at[y_hi, :, x, y_lo, q1]
        c = push(line, line, m_send.at[0, d], m_recv.at[0, d], x_peer[d])
        c.start()
        m_out.append(c)
    for d in range(1, NY):
        line = gathered.at[y_hi, :, x, y_lo, q2]
        c = push(line, line, m_send.at[1, d], m_recv.at[1, d], y_peer[d])
        c.start()
        m_out.append(c)
    lax.fori_loop(5, 8, steer, 0)
    for d in range(1, NX):
        line = gathered.at[y_hi, :, (x + NX - d) % NX, y_lo, q1]
        push(line, line, m_send.at[0, d], m_recv.at[0, d], x_peer[d]).wait_recv()
    for d in range(1, NY):
        yy = (y + NY - d) % NY
        line = gathered.at[yy // 2, :, x, yy % 2, q2]
        push(line, line, m_send.at[1, d], m_recv.at[1, d], y_peer[d]).wait_recv()

    def plane1(yy):
        return gathered.at[yy // 2, :, :, yy % 2, q1]

    def plane2(xx):
        return gathered.at[:, :, xx, :, q2]

    def plane1_in(yy):
        return gathered.at[yy // 2, :, :, yy % 2, 2 * (1 - core)]

    def plane2_in(xx):
        return gathered.at[:, :, xx, :, 2 * (1 - core) + 1]

    l_out = []
    for d in range(1, NY):
        c = push(plane1(y), plane1(y), l_send.at[0, d], l_recv.at[0, d], y_peer[d])
        c.start()
        l_out.append(c)
        c = push(plane2(x), plane2(x), l_send.at[1, d], l_recv.at[1, d], x_peer[d])
        c.start()
        l_out.append(c)
    f_out = []

    def forward(d):
        yy, xx = (y + NY - d) % NY, (x + NX - d) % NX
        for k, p in ((0, plane1(yy)), (1, plane2(xx))):
            c = push(p, p, f_send.at[k, d], f_recv.at[k, d], sibling)
            c.start()
            f_out.append(c)

    forward(0)
    lax.fori_loop(8, 16, steer, 0)
    for d in (1, 3, 2):
        yy, xx = (y + NY - d) % NY, (x + NX - d) % NX
        push(plane1(yy), plane1(yy), l_send.at[0, d], l_recv.at[0, d], y_peer[d]).wait_recv()
        push(plane2(xx), plane2(xx), l_send.at[1, d], l_recv.at[1, d], x_peer[d]).wait_recv()
        forward(d)
    for d in range(NY):
        yy, xx = (y + NY - d) % NY, (x + NX - d) % NX
        p = plane1_in(yy)
        push(p, p, f_send.at[0, d], f_recv.at[0, d], sibling).wait_recv()
        p = plane2_in(xx)
        push(p, p, f_send.at[1, d], f_recv.at[1, d], sibling).wait_recv()

    accp[...] = jnp.zeros_like(accp)
    accq[...] = jnp.zeros_like(accq)
    groups = cosb.shape[0]
    zs = NZ // groups

    def beams(g, carry):
        left = gathered[0, pl.ds(g * zs, zs)].reshape(cosb.shape[2], 128)
        right = gathered[1, pl.ds(g * zs, zs)].reshape(cosb.shape[2], 128)
        spectra = jnp.concatenate([left, right], axis=1)
        accp[...] += jnp.dot(cosb[g], spectra, preferred_element_type=F32)
        accq[...] += jnp.dot(sinb[g], spectra, preferred_element_type=F32)
        return carry

    lax.fori_loop(0, groups, beams, 0)

    sign = jnp.where(lax.broadcasted_iota(jnp.int32, (width, 128), 1) < 64, -1.0, 1.0)
    power = jnp.zeros((width, 128), F32)
    for k in range(2):
        cols = pl.ds(k * 128, 128)
        b = accp[:, cols] + sign * pltpu.roll(accq[:, cols], 64, 1)
        power = power + b * b
    scale = 1.0 / (seg_dev * lax.axis_size("seg") * mic_dev * lax.axis_size("mic") * 0.375 * samples)
    out_ref[...] = jnp.sum(power.T, axis=0, keepdims=True) * scale

    pair_done = []
    for c in z_out + m_out + l_out + f_out + pair_done:
        c.wait_send()


def shards(time_data, order_bin, mic_pos, grid_pos):
    seg_dev, mic_dev, samples = time_data.shape
    width = grid_pos.shape[1] // lax.axis_size("seg")
    mics = mic_pos.shape[1]
    chunks = 8
    dma = pltpu.SemaphoreType.DMA
    return pl.pallas_call(
        kernel,
        out_shape=jax.ShapeDtypeStruct((1, width), F32),
        in_specs=[
            pl.BlockSpec(memory_space=pl.ANY),
            pl.BlockSpec(memory_space=pltpu.SMEM),
            pl.BlockSpec(memory_space=pltpu.VMEM),
            pl.BlockSpec(memory_space=pltpu.VMEM),
        ],
        out_specs=pl.BlockSpec(memory_space=pltpu.VMEM),
        scratch_shapes=[
            pltpu.VMEM((chunks, seg_dev // chunks, mic_dev, samples), BF16),
            pltpu.VMEM((128, samples), BF16),
            pltpu.VMEM((4, 16, 128), BF16),
            pltpu.VMEM((2, 16, 128), BF16),
            pltpu.VMEM((2, NZ, NX, 2, 4, 16, 128), BF16),
            pltpu.VMEM((4, width, mics // 4), BF16),
            pltpu.VMEM((4, width, mics // 4), BF16),
            pltpu.VMEM((width, 256), F32),
            pltpu.VMEM((width, 256), F32),
            pltpu.VMEM((32, mics), BF16),
            pltpu.VMEM((width, 32), BF16),
            dma((chunks,)),
            dma, dma,
            dma((NZ,)), dma((NZ,)),
            dma((2, NX)), dma((2, NX)),
            dma((2, NX)), dma((2, NX)),
            dma((2, NX)), dma((2, NX)),
        ],
        compiler_params=pltpu.CompilerParams(
            collective_id=0, has_side_effects=True, vmem_limit_bytes=48 << 20
        ),
        name="beamform",
    )(time_data, order_bin, mic_pos, grid_pos)


def solution(mesh):
    placed = (P("seg", "mic", None), P(), P(), P(None, "mic"))
    return jax.shard_map(
        shards, mesh=mesh, in_specs=placed, out_specs=P("mic", "seg"), check_vma=False
    )
```

time: 472 us -> 38.2 us (0.08)
  other arithmetic: 265 us -> 0 us
  blocking collectives: 179 us -> 0 us
  Pallas kernels: 0 us -> 32.9 us
  matrix products: 14.5 us -> 0 us
  local copies, waits for them, and re-layouts: 11.7 us -> 4.36 us
    another operation x3 -> x0, other arithmetic: 233 us -> none
    all_gather x1 -> x0, blocking collectives: 145 us -> none  [shards(): lax.all_gather(spectra, 'mic', axis=2, tiled=True)]
    unnamed x1 -> x0, blocking collectives: 34.3 us -> none
    pallas_call x0 -> x1, Pallas kernels: none -> 32.9 us  [shards(): pl.pallas_call(kernel, out_shape=jax.ShapeDtypeStruct((1, width), F32), i...]
    mul x1 -> x0, other arithmetic: 32.1 us -> none  [beam_block(): (points[:, None, :] - mic_part[:, :, None]).astype(jnp.float32) * 0.001]
    dot_general x2 -> x0, matrix products: 14.5 us -> none  [the longest x1 12.7 us: beam_block(): return jnp.dot(left, steering, preferred_element_type=jnp.float32)]
where the time goes in v1:
time: 38.2 us; the launch traced here: 37.9 us
  Pallas kernels  32.9 us (86%)
  local copies, waits for them, and re-layouts  4.36 us (11%)
  between operations  0.67 us (2%)
    pallas_call x1, Pallas kernels, shards(): pl.pallas_call(kernel, out_shape=jax.ShapeDtypeStruct((1, width), F32), i...  32.9 us
    unnamed x7, local copies, waits for them, and re-layouts  4.36 us

profile of v1, /device:TPU:1, one launch (start us, length us, event | category | flops | bytes accessed | tf_op | source)
XLA Modules:
  0.0 37.9 jit_solution(9568394389739106006)
XLA Ops:
  0.7 0.0 copy-start
  0.7 2.2 %copy-done = bf16[32,64,1024]{2,1,0:T(8,128)(2,1)S(1)} copy-done((bf16[32,64,1024]{2,1,0:T(8,128)(2,1)S(1)}, bf16[32,64,1024]{2,1,0:T(8,128)(2,1)}, u32[]{:S(2)}) %copy-start) | copy-done | bytes 4194328
  2.8 0.0 copy-start.1
  2.8 0.8 %copy-done.1 = s32[3,4096]{1,0:T(4,128)S(1)} copy-done((s32[3,4096]{1,0:T(4,128)S(1)}, s32[3,4096]{1,0:T(4,128)}, u32[]{:S(2)}) %copy-start.1) | copy-done | bytes 49176
  3.7 0.0 copy-start.2
  3.7 0.8 %copy-done.2 = s32[3,2048]{1,0:T(4,128)S(1)} copy-done((s32[3,2048]{1,0:T(4,128)S(1)}, s32[3,2048]{1,0:T(4,128)}, u32[]{:S(2)}) %copy-start.2) | copy-done | bytes 24600
  4.4 32.9 %beamform.1 = f32[1,512]{1,0:T(1,128)S(1)} custom-call(bf16[32,64,1024]{2,1,0:T(8,128)(2,1)S(1)} %copy-done, s32[1]{0:T(128)S(6)} %copy.6.bin_ref, s32[3,4096]{1,0:T(4,128)S(1)} %copy-done.1, s32[3,2048]{1,0:T(4,128)S(1)} %copy-done.2), custom_call_target="tpu_custom_call" | custom-call | tf_op jit(solution)/shard_map/beamform/pallas_call | solution.py:270
  37.4 0.6 %copy.7 = f32[1,512]{1,0:T(1,128)} copy(f32[1,512]{1,0:T(1,128)S(1)} %beamform.1) | data formatting | bytes 4096
Async XLA Ops:
  0.7 2.2 %copy-start = (bf16[32,64,1024]{2,1,0:T(8,128)(2,1)S(1)}, bf16[32,64,1024]{2,1,0:T(8,128)(2,1)}, u32[]{:S(2)}) copy-start(bf16[32,64,1024]{2,1,0:T(8,128)(2,1)} %time_ref.1) | copy-start | bytes 12582916
  2.8 0.8 %copy-start.1 = (s32[3,4096]{1,0:T(4,128)S(1)}, s32[3,4096]{1,0:T(4,128)}, u32[]{:S(2)}) copy-start(s32[3,4096]{1,0:T(4,128)} %mic_ref.1) | copy-start | bytes 147460
  3.7 0.8 %copy-start.2 = (s32[3,2048]{1,0:T(4,128)S(1)}, s32[3,2048]{1,0:T(4,128)}, u32[]{:S(2)}) copy-start(s32[3,2048]{1,0:T(4,128)} %grid_ref.1) | copy-start | bytes 73732

commit v2 on v0

v2 whole, which is shorter than its diff:
```python
import functools
import math

import jax
import jax.numpy as jnp
from jax import lax
from jax.experimental import pallas as pl
from jax.experimental.pallas import tpu as pltpu
from jax.sharding import PartitionSpec as P

MESH = pl.DeviceIdType.MESH
F32 = jnp.float32
BF16 = jnp.bfloat16

NX, NY, NZ = 4, 4, 8
AT_LINES, AT_PLANES, AT_BEAMS = 2, 7, 13
SIN = (4.442882834149665, -7.308241154529405, 3.6062889579421076, -0.8457635944249917, 0.10920575020378133)
COS = (1.414213496564824, -6.978850988209009, 5.739461169968767, -1.8835629820109427, 0.3106981797730274)
SIN_SHORT = (4.442867902991959, -7.3074434197428175, 3.5947880638880885, -0.7843739922969518)
COS_SHORT = (1.4142040804388327, -6.977642054046934, 5.715238359077324, -1.728348549561637)


def horner(coefs, z):
    total = jnp.full_like(z, coefs[-1])
    for c in coefs[-2::-1]:
        total = total * z + c
    return total


def cos_sin_turns(turns, sin_coefs, cos_coefs):
    r = turns - jnp.round(turns)
    z = r * r
    s = r * horner(sin_coefs, z)
    c = horner(cos_coefs, z)
    return 1.0 - s * s, s * c


def device(y, z, x, core):
    return {"seg": (y // 2) * 2 + core, "mic": (z * NX + x) * 2 + y % 2}


def kernel(
    time_ref, bin_ref, mic_hbm, grid_hbm, out_ref,
    mic_ref, grid_ref, s_sem, tbuf, wt, own, kept, inbox, gathered, cosb, sinb, accp, accq, sent, received, micf, pointf,
    t_sem, p_send, p_recv, z_send, z_recv, m_send, m_recv, l_send, l_recv, b_send, b_recv,
):
    seg = lax.axis_index("seg")
    mic = lax.axis_index("mic")
    core = seg % 2
    y_hi, y_lo = seg // 2, mic % 2
    y = y_hi * 2 + y_lo
    x = (mic // 2) % NX
    z = mic // (2 * NX)
    zp = z // 2
    sibling = device(y, z, x, 1 - core)
    z_peer = [device(y, (z + d) % NZ, x, core) for d in range(NZ)]
    x_peer = [device(y, z, (x + d) % NX, core) for d in range(NX)]
    y_peer = [device((y + d) % NY, z, x, core) for d in range(NY)]

    seg_dev, mic_dev, samples = time_ref.shape
    mic_half = mic_dev // 2
    chunks, per = tbuf.shape[0], tbuf.shape[1]

    def time_copy(i):
        side = (1 - core) if i < chunks // 2 else core
        first = (i % (chunks // 2)) * per
        src = time_ref.at[pl.ds(first, per), pl.ds(side * mic_half, mic_half)]
        return pltpu.make_async_copy(src, tbuf.at[i], t_sem.at[i])

    small = [
        pltpu.make_async_copy(src, dst, s_sem.at[i])
        for i, (src, dst) in enumerate(((mic_hbm, mic_ref), (grid_hbm, grid_ref)))
    ]
    for c in small:
        c.start()
    for i in range(chunks):
        time_copy(i).start()

    barrier = pltpu.get_barrier_semaphore()
    peers = [sibling] + z_peer[1:] + x_peer[1:] + y_peer[1:]
    for peer in peers:
        pl.semaphore_signal(barrier, inc=1, device_id=peer, device_id_type=MESH)

    order = bin_ref[0]
    t = lax.broadcasted_iota(jnp.int32, (8, samples), 1)
    turned = (order * t) & (samples - 1)
    inv = 1.0 / samples
    wcos, _ = cos_sin_turns(t.astype(F32) * inv, SIN, COS)
    ca, sa = cos_sin_turns(turned.astype(F32) * inv, SIN, COS)
    window = 0.5 - 0.5 * wcos
    rows = jnp.concatenate([window * ca] * 8 + [-(window * sa)] * 8, axis=0)
    wt[...] = rows.T.astype(BF16)

    lane = lax.broadcasted_iota(jnp.int32, (mic_half, 128), 1) & 63

    def spectra(first_chunk):
        acc = jnp.zeros((mic_half, 128), F32)
        for i in range(chunks // 2):
            time_copy(first_chunk + i).wait()
            part = jnp.dot(
                tbuf[first_chunk + i].reshape(per * mic_half, samples), wt[...], preferred_element_type=F32
            )
            for k in range(per):
                hit = lane == core * seg_dev + i * per + k
                acc = jnp.where(hit, part[k * mic_half:(k + 1) * mic_half], acc)
        return acc.astype(BF16).reshape(2, 16, 128)

    def push(src, dst, send, recv, peer):
        return pltpu.make_async_remote_copy(
            src_ref=src, dst_ref=dst, send_sem=send, recv_sem=recv, device_id=peer, device_id_type=MESH
        )

    own[...] = spectra(0)
    kept[...] = spectra(chunks // 2)
    pair_copy = push(own, inbox, p_send, p_recv, sibling)
    pl.semaphore_wait(barrier, len(peers))
    pair_copy.start()
    accp[...] = jnp.zeros_like(accp)
    accq[...] = jnp.zeros_like(accq)

    def split(v):
        coarse = jnp.floor(v * (1.0 / 64.0) + 0.5) * 64.0
        return coarse, v - coarse

    def split3(v):
        top = jnp.floor(v * (1.0 / 65536.0)) * 65536.0
        rest = v - top
        mid = jnp.floor(rest * (1.0 / 256.0)) * 256.0
        return top, mid, rest - mid

    def rows_of(v, fold):
        hi, lo = split(v)
        sq = v * v
        top, mid, low = split3(sq[0:1] + sq[1:2] + sq[2:3])
        one = jnp.ones_like(top)
        tiny = jnp.full_like(top, 2.0**-20)
        zero = jnp.zeros((13, v.shape[1]), F32)
        if fold:
            return jnp.concatenate([-2.0 * hi, -2.0 * hi, -2.0 * lo, -2.0 * lo, one, one, one, top, mid, low, tiny, zero], axis=0)
        return jnp.concatenate([hi, lo, hi, lo, top, mid, low, one, one, one, tiny, zero], axis=0)

    for c in small:
        c.wait()
    width = out_ref.shape[1]
    pts = grid_ref[:, pl.ds(pl.multiple_of(y_hi * 2 * width, 128), 2 * width)].astype(F32)
    pointf[...] = rows_of(pts, False).T.astype(BF16)
    mine = gathered.at[y_hi, z, x, y_lo]

    def z_copy(d):
        return push(mine, mine, z_send.at[d], z_recv.at[z], z_peer[d])

    pair_copy.wait_recv()
    mine[...] = kept[...] + inbox[...]
    for d in (4, 3, 5, 2, 6, 1, 7):
        z_copy(d).start()

    every = rows_of(mic_ref[...].astype(F32), True).astype(BF16)
    part = 8 * mic_dev
    parts = every.shape[1] // part
    stacked = jnp.concatenate([every[:, i * part:(i + 1) * part] for i in range(parts)], axis=0)
    src = lax.broadcasted_iota(jnp.int32, (part, part // 2), 0)
    dst = lax.broadcasted_iota(jnp.int32, (part, part // 2), 1)
    wanted = (dst // mic_half) * mic_dev + core * mic_half + (dst & (mic_half - 1))
    pick = jnp.where(src == wanted, 1.0, 0.0).astype(BF16)
    picked = jnp.dot(stacked, pick, preferred_element_type=F32).astype(BF16)
    micf[...] = jnp.concatenate([picked[i * 32:(i + 1) * 32] for i in range(parts)], axis=1)
    turns_per_mm = order.astype(F32) * F32(0.001 * 51200.0 / 343.0 / samples)

    groups, depth = cosb.shape[0], cosb.shape[2]
    blocks = 4
    tall = 128

    def pair(k):
        return (zp + k * (k + 1) // 2) % groups

    def steer(j):
        g = pair(j // blocks)
        feat = micf[:, pl.ds(pl.multiple_of(g * depth, depth), depth)]
        span = 2 * width // blocks
        for i in range(span // tall):
            rows = pl.ds(pl.multiple_of((j % blocks) * span + i * tall, tall), tall)
            d2 = jnp.dot(pointf[rows, :], feat, preferred_element_type=F32)
            turns = (d2 * turns_per_mm) * lax.rsqrt(d2)
            ca, sa = cos_sin_turns(turns, SIN_SHORT, COS_SHORT)
            cosb[g, rows, :] = ca.astype(BF16)
            sinb[g, rows, :] = sa.astype(BF16)

    q1, q2 = 0, 1

    def line(k, yy, xx, q):
        return gathered.at[yy // 2, pl.ds(2 * pair(k), 2), xx, yy % 2, q]

    def plane1(k, yy):
        return gathered.at[yy // 2, pl.ds(2 * pair(k), 2), :, yy % 2, q1]

    def plane2(k, xx):
        return gathered.at[:, pl.ds(2 * pair(k), 2), xx, :, q2]

    def z_arrived(k):
        for b in range(2):
            zz = 2 * pair(k) + b

            @pl.when(zz != z)
            def _():
                src = gathered.at[y_hi, zz, x, y_lo]
                push(src, src, z_send.at[1], z_recv.at[zz], z_peer[1]).wait_recv()

    def line_copies(k, d, back):
        xx, yy = ((x + NX - d) % NX, (y + NY - d) % NY) if back else (x, y)
        p1, p2 = line(k, y, xx, q1), line(k, yy, x, q2)
        return (
            push(p1, p1, m_send.at[0, k, d], m_recv.at[0, k, d], x_peer[d]),
            push(p2, p2, m_send.at[1, k, d], m_recv.at[1, k, d], y_peer[d]),
        )

    def plane_copies(k, d, back):
        xx, yy = ((x + NX - d) % NX, (y + NY - d) % NY) if back else (x, y)
        p1, p2 = plane1(k, yy), plane2(k, xx)
        return (
            push(p1, p1, l_send.at[0, k, d], l_recv.at[0, k, d], y_peer[d]),
            push(p2, p2, l_send.at[1, k, d], l_recv.at[1, k, d], x_peer[d]),
        )

    def begin(copies, k):
        for d in (2, 1, 3):
            for c in copies(k, d, False):
                c.start()

    def arrived(copies, k):
        for d in (1, 3, 2):
            for c in copies(k, d, True):
                c.wait_recv()

    def flown(copies, k):
        for d in (1, 3, 2):
            for c in copies(k, d, False):
                c.wait_send()

    piece = width // 2

    sign = jnp.where(lax.broadcasted_iota(jnp.int32, (piece, 128), 1) < 64, -1.0, 1.0)

    def rows_at(side, r):
        return pl.ds(pl.multiple_of(side * width + r * piece, piece), piece)

    def beam_copy(r):
        return push(sent.at[r], received.at[r], b_send.at[r], b_recv.at[r], sibling)

    def combined(rows, c):
        cols = pl.ds(c * 128, 128)
        return accp[rows, cols] + sign * pltpu.roll(accq[rows, cols], 64, 1)

    def beams(k, rows):
        g = pair(k)
        zs = pl.ds(2 * g, 2)
        low = gathered[0, zs].reshape(depth, 128)
        high = gathered[1, zs].reshape(depth, 128)
        spec = jnp.concatenate([low, high], axis=1)
        accp[rows, :] += jnp.dot(cosb[g, rows, :], spec, preferred_element_type=F32)
        accq[rows, :] += jnp.dot(sinb[g, rows, :], spec, preferred_element_type=F32)

    steps = groups * blocks

    def step(j, carry):
        pl.when(j < steps)(lambda: steer(j))

        @pl.when((j >= AT_LINES) & (j < AT_LINES + groups))
        def _():
            z_arrived(j - AT_LINES)
            begin(line_copies, j - AT_LINES)

        @pl.when((j >= AT_PLANES) & (j < AT_PLANES + groups))
        def _():
            arrived(line_copies, j - AT_PLANES)
            begin(plane_copies, j - AT_PLANES)

        @pl.when((j >= AT_BEAMS) & (j < AT_BEAMS + groups))
        def _():
            arrived(plane_copies, j - AT_BEAMS)
            def theirs(r, carry):
                rows = rows_at(1 - core, r)
                beams(j - AT_BEAMS, rows)

                @pl.when(j == AT_BEAMS + groups - 1)
                def _():
                    for c in range(2):
                        sent[r, :, pl.ds(c * 128, 128)] = combined(rows, c)
                    beam_copy(r).start()

                return carry

            lax.fori_loop(0, 2, theirs, 0)
            beams(j - AT_BEAMS, pl.ds(pl.multiple_of(core * width, width), width))

        return carry

    lax.fori_loop(0, AT_BEAMS + groups, step, 0)

    scale = 1.0 / (seg_dev * lax.axis_size("seg") * mic_dev * lax.axis_size("mic") * 0.375 * samples)
    for r in range(2):
        mixed = [combined(rows_at(core, r), c) for c in range(2)]
        beam_copy(r).wait_recv()
        power = jnp.zeros((piece, 128), F32)
        for c in range(2):
            b = mixed[c] + received[r, :, pl.ds(c * 128, 128)]
            power = power + b * b
        out_ref[:, pl.ds(r * piece, piece)] = jnp.sum(power.T, axis=0, keepdims=True) * scale

    pair_copy.wait_send()
    for r in range(2):
        beam_copy(r).wait_send()
    for d in range(1, NZ):
        z_copy(d).wait_send()

    def drain(k, carry):
        flown(line_copies, k)
        flown(plane_copies, k)
        return carry

    lax.fori_loop(0, groups, drain, 0)


def shards(time_data, order_bin, mic_pos, grid_pos):
    seg_dev, mic_dev, samples = time_data.shape
    width = grid_pos.shape[1] // lax.axis_size("seg")
    mics = mic_pos.shape[1]
    chunks = 4
    dma = pltpu.SemaphoreType.DMA
    return pl.pallas_call(
        kernel,
        out_shape=jax.ShapeDtypeStruct((1, width), F32),
        in_specs=[
            pl.BlockSpec(memory_space=pltpu.HBM),
            pl.BlockSpec(memory_space=pltpu.SMEM),
            pl.BlockSpec(memory_space=pltpu.HBM),
            pl.BlockSpec(memory_space=pltpu.HBM),
        ],
        out_specs=pl.BlockSpec(memory_space=pltpu.VMEM),
        scratch_shapes=[
            pltpu.VMEM(mic_pos.shape, jnp.int32),
            pltpu.VMEM(grid_pos.shape, jnp.int32),
            pltpu.SemaphoreType.DMA((2,)),
            pltpu.VMEM((chunks, 2 * seg_dev // chunks, mic_dev // 2, samples), BF16),
            pltpu.VMEM((samples, 128), BF16),
            pltpu.VMEM((2, 16, 128), BF16),
            pltpu.VMEM((2, 16, 128), BF16),
            pltpu.VMEM((2, 16, 128), BF16),
            pltpu.VMEM((2, NZ, NX, 2, 2, 16, 128), BF16),
            pltpu.VMEM((4, 2 * width, mics // 8), BF16),
            pltpu.VMEM((4, 2 * width, mics // 8), BF16),
            pltpu.VMEM((2 * width, 256), F32),
            pltpu.VMEM((2 * width, 256), F32),
            pltpu.VMEM((2, width // 2, 256), F32),
            pltpu.VMEM((2, width // 2, 256), F32),
            pltpu.VMEM((32, mics // 2), BF16),
            pltpu.VMEM((2 * width, 32), BF16),
            dma((chunks,)),
            dma, dma,
            dma((NZ,)), dma((NZ,)),
            dma((2, 4, NX)), dma((2, 4, NX)),
            dma((2, 4, NX)), dma((2, 4, NX)),
            dma((2,)), dma((2,)),
        ],
        compiler_params=pltpu.CompilerParams(
            collective_id=0, has_side_effects=True, vmem_limit_bytes=55208 << 10
        ),
        name="beamform",
    )(time_data, order_bin, mic_pos, grid_pos)


def solution(mesh):
    placed = (P("seg", "mic", None), P(), P(), P(None, "mic"))
    return jax.shard_map(
        shards, mesh=mesh, in_specs=placed, out_specs=P("mic", "seg"), check_vma=False
    )
```

time: 472 us -> 32.2 us (0.07)
  other arithmetic: 265 us -> 0 us
  blocking collectives: 179 us -> 0 us
  Pallas kernels: 0 us -> 30.9 us
  matrix products: 14.5 us -> 0 us
  local copies, waits for them, and re-layouts: 11.7 us -> 0.58 us
    another operation x3 -> x0, other arithmetic: 233 us -> none
    all_gather x1 -> x0, blocking collectives: 145 us -> none  [shards(): lax.all_gather(spectra, 'mic', axis=2, tiled=True)]
    unnamed x1 -> x0, blocking collectives: 34.3 us -> none
    mul x1 -> x0, other arithmetic: 32.1 us -> none  [beam_block(): (points[:, None, :] - mic_part[:, :, None]).astype(jnp.float32) * 0.001]
    pallas_call x0 -> x1, Pallas kernels: none -> 30.9 us  [shards(): pl.pallas_call(kernel, out_shape=jax.ShapeDtypeStruct((1, width), F32), i...]
    dot_general x2 -> x0, matrix products: 14.5 us -> none  [the longest x1 12.7 us: beam_block(): return jnp.dot(left, steering, preferred_element_type=jnp.float32)]
    unnamed x8 -> x1, local copies, waits for them, and re-layouts: 7.81 us -> 0.58 us
where the time goes in v2:
time: 32.2 us; the launch traced here: 32.1 us
  Pallas kernels  30.9 us (96%)
  between operations  0.66 us (2%)
  local copies, waits for them, and re-layouts  0.58 us (2%)
    pallas_call x1, Pallas kernels, shards(): pl.pallas_call(kernel, out_shape=jax.ShapeDtypeStruct((1, width), F32), i...  30.9 us

profile of v2, /device:TPU:1, one launch (start us, length us, event | category | flops | bytes accessed | tf_op | source)
XLA Modules:
  0.0 32.1 jit_solution(11145898492558772897)
XLA Ops:
  0.7 30.9 %beamform.1 = f32[1,512]{1,0:T(1,128)S(1)} custom-call(bf16[32,64,1024]{2,1,0:T(8,128)(2,1)} %time_ref.1, s32[1]{0:T(128)S(6)} %copy.6.bin_ref, s32[3,4096]{1,0:T(4,128)} %mic_hbm.1, s32[3,2048]{1,0:T(4,128)} %grid_hbm.1), custom_call_target="tpu_custom_call" | custom-call | tf_op jit(solution)/shard_map/beamform/pallas_call | solution.py:329
  31.5 0.6 %copy.7 = f32[1,512]{1,0:T(1,128)} copy(f32[1,512]{1,0:T(1,128)S(1)} %beamform.1) | data formatting | bytes 4096

commit v3 on v2

--- a/solution.py
+++ b/solution.py
@@ -13,7 +13,9 @@
 BF16 = jnp.bfloat16
 
 NX, NY, NZ = 4, 4, 8
-AT_LINES, AT_PLANES, AT_BEAMS = 2, 7, 13
+BLOCKS = 2
+LINES, PLANES, BEAMS = (1,2,2,3), (4,4,5,5), (8,8,8,8)
+CHUNKS, AHEAD = 4, 4
 SIN = (4.442882834149665, -7.308241154529405, 3.6062889579421076, -0.8457635944249917, 0.10920575020378133)
 COS = (1.414213496564824, -6.978850988209009, 5.739461169968767, -1.8835629820109427, 0.3106981797730274)
 SIN_SHORT = (4.442867902991959, -7.3074434197428175, 3.5947880638880885, -0.7843739922969518)
@@ -41,7 +43,7 @@
 
 def kernel(
     time_ref, bin_ref, mic_hbm, grid_hbm, out_ref,
-    mic_ref, grid_ref, s_sem, tbuf, wt, own, kept, inbox, gathered, cosb, sinb, accp, accq, sent, received, micf, pointf,
+    mic_ref, grid_ref, s_sem, tbuf, wt, own, kept, inbox, gathered, steering, acc, right, sent, received, micf, pointf,
     t_sem, p_send, p_recv, z_send, z_recv, m_send, m_recv, l_send, l_recv, b_send, b_recv,
 ):
     seg = lax.axis_index("seg")
@@ -73,7 +75,8 @@
     ]
     for c in small:
         c.start()
-    for i in range(chunks):
+    ahead = AHEAD
+    for i in range(ahead):
         time_copy(i).start()
 
     barrier = pltpu.get_barrier_semaphore()
@@ -94,16 +97,18 @@
     lane = lax.broadcasted_iota(jnp.int32, (mic_half, 128), 1) & 63
 
     def spectra(first_chunk):
-        acc = jnp.zeros((mic_half, 128), F32)
+        own_sum = jnp.zeros((mic_half, 128), F32)
         for i in range(chunks // 2):
             time_copy(first_chunk + i).wait()
+            if first_chunk + i + ahead < chunks:
+                time_copy(first_chunk + i + ahead).start()
             part = jnp.dot(
                 tbuf[first_chunk + i].reshape(per * mic_half, samples), wt[...], preferred_element_type=F32
             )
             for k in range(per):
                 hit = lane == core * seg_dev + i * per + k
-                acc = jnp.where(hit, part[k * mic_half:(k + 1) * mic_half], acc)
-        return acc.astype(BF16).reshape(2, 16, 128)
+                own_sum = jnp.where(hit, part[k * mic_half:(k + 1) * mic_half], own_sum)
+        return own_sum.astype(BF16).reshape(2, 16, 128)
 
     def push(src, dst, send, recv, peer):
         return pltpu.make_async_remote_copy(
@@ -115,8 +120,7 @@
     pair_copy = push(own, inbox, p_send, p_recv, sibling)
     pl.semaphore_wait(barrier, len(peers))
     pair_copy.start()
-    accp[...] = jnp.zeros_like(accp)
-    accq[...] = jnp.zeros_like(accq)
+    acc[...] = jnp.zeros_like(acc)
 
     def split(v):
         coarse = jnp.floor(v * (1.0 / 64.0) + 0.5) * 64.0
@@ -166,8 +170,8 @@
     micf[...] = jnp.concatenate([picked[i * 32:(i + 1) * 32] for i in range(parts)], axis=1)
     turns_per_mm = order.astype(F32) * F32(0.001 * 51200.0 / 343.0 / samples)
 
-    groups, depth = cosb.shape[0], cosb.shape[2]
-    blocks = 4
+    groups, depth = steering.shape[0], steering.shape[2] // 2
+    blocks = BLOCKS
     tall = 128
 
     def pair(k):
@@ -182,8 +186,8 @@
             d2 = jnp.dot(pointf[rows, :], feat, preferred_element_type=F32)
             turns = (d2 * turns_per_mm) * lax.rsqrt(d2)
             ca, sa = cos_sin_turns(turns, SIN_SHORT, COS_SHORT)
-            cosb[g, rows, :] = ca.astype(BF16)
-            sinb[g, rows, :] = sa.astype(BF16)
+            steering[g, rows, pl.ds(0, depth)] = ca.astype(BF16)
+            steering[g, rows, pl.ds(depth, depth)] = sa.astype(BF16)
 
     q1, q2 = 0, 1
 
@@ -238,72 +242,87 @@
 
     piece = width // 2
 
-    sign = jnp.where(lax.broadcasted_iota(jnp.int32, (piece, 128), 1) < 64, -1.0, 1.0)
-
     def rows_at(side, r):
         return pl.ds(pl.multiple_of(side * width + r * piece, piece), piece)
 
     def beam_copy(r):
         return push(sent.at[r], received.at[r], b_send.at[r], b_recv.at[r], sibling)
 
-    def combined(rows, c):
-        cols = pl.ds(c * 128, 128)
-        return accp[rows, cols] + sign * pltpu.roll(accq[rows, cols], 64, 1)
+    def turned_spectra(k):
+        zs = pl.ds(2 * pair(k), 2)
+        sides = [gathered[h, zs].reshape(depth, 128) for h in range(2)]
+        sign = jnp.where(lax.broadcasted_iota(jnp.int32, (depth, 128), 1) < 64, -1.0, 1.0)
+        turned = [(pltpu.roll(v.astype(F32), 64, 1) * sign).astype(BF16) for v in sides]
+        right[...] = jnp.concatenate(
+            [jnp.concatenate(sides, axis=1), jnp.concatenate(turned, axis=1)], axis=0
+        )
 
     def beams(k, rows):
-        g = pair(k)
-        zs = pl.ds(2 * g, 2)
-        low = gathered[0, zs].reshape(depth, 128)
-        high = gathered[1, zs].reshape(depth, 128)
-        spec = jnp.concatenate([low, high], axis=1)
-        accp[rows, :] += jnp.dot(cosb[g, rows, :], spec, preferred_element_type=F32)
-        accq[rows, :] += jnp.dot(sinb[g, rows, :], spec, preferred_element_type=F32)
+        return acc[rows, :] + jnp.dot(steering[pair(k), rows, :], right[...], preferred_element_type=F32)
 
     steps = groups * blocks
+
+    def at_step(j, when, event):
+        first = sum(jnp.where(j > w, 1, 0) for w in when)
+        last = sum(jnp.where(j >= w, 1, 0) for w in when)
+
+        def body(k, carry):
+            event(k)
+            return carry
+
+        lax.fori_loop(first, last, body, 0)
+
+    def lines_event(k):
+        z_arrived(k)
+        begin(line_copies, k)
+
+    def planes_event(k):
+        arrived(line_copies, k)
+        begin(plane_copies, k)
+
+    def beams_event(k):
+        arrived(plane_copies, k)
+        turned_spectra(k)
+
+        def theirs(r, carry):
+            rows = rows_at(1 - core, r)
+            total = beams(k, rows)
+
+            @pl.when(k < groups - 1)
+            def _():
+                acc[rows, :] = total
+
+            @pl.when(k == groups - 1)
+            def _():
+                sent[r] = total
+                beam_copy(r).start()
+
+            return carry
+
+        lax.fori_loop(0, 2, theirs, 0)
+
+        def ours(r, carry):
+            rows = rows_at(core, r)
+            acc[rows, :] = beams(k, rows)
+            return carry
+
+        lax.fori_loop(0, 2, ours, 0)
 
     def step(j, carry):
         pl.when(j < steps)(lambda: steer(j))
-
-        @pl.when((j >= AT_LINES) & (j < AT_LINES + groups))
-        def _():
-            z_arrived(j - AT_LINES)
-            begin(line_copies, j - AT_LINES)
-
-        @pl.when((j >= AT_PLANES) & (j < AT_PLANES + groups))
-        def _():
-            arrived(line_copies, j - AT_PLANES)
-            begin(plane_copies, j - AT_PLANES)
-
-        @pl.when((j >= AT_BEAMS) & (j < AT_BEAMS + groups))
-        def _():
-            arrived(plane_copies, j - AT_BEAMS)
-            def theirs(r, carry):
-                rows = rows_at(1 - core, r)
-                beams(j - AT_BEAMS, rows)
-
-                @pl.when(j == AT_BEAMS + groups - 1)
-                def _():
-                    for c in range(2):
-                        sent[r, :, pl.ds(c * 128, 128)] = combined(rows, c)
-                    beam_copy(r).start()
-
-                return carry
-
-            lax.fori_loop(0, 2, theirs, 0)
-            beams(j - AT_BEAMS, pl.ds(pl.multiple_of(core * width, width), width))
-
+        at_step(j, LINES, lines_event)
+        at_step(j, PLANES, planes_event)
+        at_step(j, BEAMS, beams_event)
         return carry
 
-    lax.fori_loop(0, AT_BEAMS + groups, step, 0)
+    lax.fori_loop(0, BEAMS[-1] + 1, step, 0)
 
     scale = 1.0 / (seg_dev * lax.axis_size("seg") * mic_dev * lax.axis_size("mic") * 0.375 * samples)
     for r in range(2):
-        mixed = [combined(rows_at(core, r), c) for c in range(2)]
         beam_copy(r).wait_recv()
-        power = jnp.zeros((piece, 128), F32)
-        for c in range(2):
-            b = mixed[c] + received[r, :, pl.ds(c * 128, 128)]
-            power = power + b * b
+        total = acc[rows_at(core, r), :] + received[r]
+        power = total * total
+        power = power[:, :128] + power[:, 128:]
         out_ref[:, pl.ds(r * piece, piece)] = jnp.sum(power.T, axis=0, keepdims=True) * scale
 
     pair_copy.wait_send()
@@ -324,7 +343,7 @@
     seg_dev, mic_dev, samples = time_data.shape
     width = grid_pos.shape[1] // lax.axis_size("seg")
     mics = mic_pos.shape[1]
-    chunks = 4
+    chunks = CHUNKS
     dma = pltpu.SemaphoreType.DMA
     return pl.pallas_call(
         kernel,
@@ -346,10 +365,9 @@
             pltpu.VMEM((2, 16, 128), BF16),
             pltpu.VMEM((2, 16, 128), BF16),
             pltpu.VMEM((2, NZ, NX, 2, 2, 16, 128), BF16),
-            pltpu.VMEM((4, 2 * width, mics // 8), BF16),
-            pltpu.VMEM((4, 2 * width, mics // 8), BF16),
+            pltpu.VMEM((4, 2 * width, mics // 4), BF16),
             pltpu.VMEM((2 * width, 256), F32),
-            pltpu.VMEM((2 * width, 256), F32),
+            pltpu.VMEM((mics // 4, 256), BF16),
             pltpu.VMEM((2, width // 2, 256), F32),
             pltpu.VMEM((2, width // 2, 256), F32),
             pltpu.VMEM((32, mics // 2), BF16),

time: 32.2 us -> 31.9 us (level)
    pallas_call x1, Pallas kernels: 30.9 us -> 30.6 us  [shards(): pl.pallas_call(kernel, out_shape=jax.ShapeDtypeStruct((1, width), F32), i...]
where the time goes in v3:
time: 31.9 us; the launch traced here: 31.8 us
  Pallas kernels  30.6 us (96%)
  between operations  0.66 us (2%)
  local copies, waits for them, and re-layouts  0.58 us (2%)
    pallas_call x1, Pallas kernels, shards(): pl.pallas_call(kernel, out_shape=jax.ShapeDtypeStruct((1, width), F32), i...  30.6 us

profile of v3, /device:TPU:1, one launch (start us, length us, event | category | flops | bytes accessed | tf_op | source)
XLA Modules:
  0.0 31.8 jit_solution(7861167514501072532)
XLA Ops:
  0.7 30.6 %beamform.1 = f32[1,512]{1,0:T(1,128)S(1)} custom-call(bf16[32,64,1024]{2,1,0:T(8,128)(2,1)} %time_ref.1, s32[1]{0:T(128)S(6)} %copy.6.bin_ref, s32[3,4096]{1,0:T(4,128)} %mic_hbm.1, s32[3,2048]{1,0:T(4,128)} %grid_hbm.1), custom_call_target="tpu_custom_call" | custom-call | tf_op jit(solution)/shard_map/beamform/pallas_call | solution.py:348
  31.2 0.6 %copy.7 = f32[1,512]{1,0:T(1,128)} copy(f32[1,512]{1,0:T(1,128)S(1)} %beamform.1) | data formatting | bytes 4096

commit v4 on v3

--- a/solution.py
+++ b/solution.py
@@ -59,6 +59,12 @@
     x_peer = [device(y, z, (x + d) % NX, core) for d in range(NX)]
     y_peer = [device((y + d) % NY, z, x, core) for d in range(NY)]
 
+    barrier = pltpu.get_barrier_semaphore()
+    peers = [z_peer[d] for d in (4, 3, 5, 2, 6)] + [x_peer[2], y_peer[2]]
+    peers += [z_peer[d] for d in (1, 7)] + [p[d] for p in (x_peer, y_peer) for d in (1, 3)] + [sibling]
+    for peer in peers:
+        pl.semaphore_signal(barrier, inc=1, device_id=peer, device_id_type=MESH)
+
     seg_dev, mic_dev, samples = time_ref.shape
     mic_half = mic_dev // 2
     chunks, per = tbuf.shape[0], tbuf.shape[1]
@@ -78,11 +84,6 @@
     ahead = AHEAD
     for i in range(ahead):
         time_copy(i).start()
-
-    barrier = pltpu.get_barrier_semaphore()
-    peers = [sibling] + z_peer[1:] + x_peer[1:] + y_peer[1:]
-    for peer in peers:
-        pl.semaphore_signal(barrier, inc=1, device_id=peer, device_id_type=MESH)
 
     order = bin_ref[0]
     t = lax.broadcasted_iota(jnp.int32, (8, samples), 1)

time: 31.9 us -> 31.8 us (level)
  no operation moved by 1% of the time
where the time goes in v4:
time: 31.8 us; the launch traced here: 31.7 us
  Pallas kernels  30.5 us (96%)
  between operations  0.66 us (2%)
  local copies, waits for them, and re-layouts  0.58 us (2%)
    pallas_call x1, Pallas kernels, shards(): pl.pallas_call(kernel, out_shape=jax.ShapeDtypeStruct((1, width), F32), i...  30.5 us

profile of v4, /device:TPU:1, one launch (start us, length us, event | category | flops | bytes accessed | tf_op | source)
XLA Modules:
  0.0 31.7 jit_solution(1797220016226556055)
XLA Ops:
  0.7 30.5 %beamform.1 = f32[1,512]{1,0:T(1,128)S(1)} custom-call(bf16[32,64,1024]{2,1,0:T(8,128)(2,1)} %time_ref.1, s32[1]{0:T(128)S(6)} %copy.6.bin_ref, s32[3,4096]{1,0:T(4,128)} %mic_hbm.1, s32[3,2048]{1,0:T(4,128)} %grid_hbm.1), custom_call_target="tpu_custom_call" | custom-call | tf_op jit(solution)/shard_map/beamform/pallas_call | solution.py:349
  31.2 0.6 %copy.7 = f32[1,512]{1,0:T(1,128)} copy(f32[1,512]{1,0:T(1,128)S(1)} %beamform.1) | data formatting | bytes 4096

commit v5 on v3

--- a/solution.py
+++ b/solution.py
@@ -15,7 +15,7 @@
 NX, NY, NZ = 4, 4, 8
 BLOCKS = 2
 LINES, PLANES, BEAMS = (1,2,2,3), (4,4,5,5), (8,8,8,8)
-CHUNKS, AHEAD = 4, 4
+CHUNKS, AHEAD = 8, 8
 SIN = (4.442882834149665, -7.308241154529405, 3.6062889579421076, -0.8457635944249917, 0.10920575020378133)
 COS = (1.414213496564824, -6.978850988209009, 5.739461169968767, -1.8835629820109427, 0.3106981797730274)
 SIN_SHORT = (4.442867902991959, -7.3074434197428175, 3.5947880638880885, -0.7843739922969518)

time: 31.9 us -> 31.9 us (level)
  no operation moved by 1% of the time
where the time goes in v5:
time: 31.9 us
  Pallas kernels  30.6 us (96%)
  between operations  0.66 us (2%)
  local copies, waits for them, and re-layouts  0.58 us (2%)
    pallas_call x1, Pallas kernels, shards(): pl.pallas_call(kernel, out_shape=jax.ShapeDtypeStruct((1, width), F32), i...  30.6 us

profile of v5, /device:TPU:1, one launch (start us, length us, event | category | flops | bytes accessed | tf_op | source)
XLA Modules:
  0.0 31.9 jit_solution(15970259424554438364)
XLA Ops:
  0.7 30.6 %beamform.1 = f32[1,512]{1,0:T(1,128)S(1)} custom-call(bf16[32,64,1024]{2,1,0:T(8,128)(2,1)} %time_ref.1, s32[1]{0:T(128)S(6)} %copy.6.bin_ref, s32[3,4096]{1,0:T(4,128)} %mic_hbm.1, s32[3,2048]{1,0:T(4,128)} %grid_hbm.1), custom_call_target="tpu_custom_call" | custom-call | tf_op jit(solution)/shard_map/beamform/pallas_call | solution.py:348
  31.3 0.6 %copy.7 = f32[1,512]{1,0:T(1,128)} copy(f32[1,512]{1,0:T(1,128)S(1)} %beamform.1) | data formatting | bytes 4096
